TPU v7x, 256 devices: a whole 4x4x8 slice. The times are simulated.
256 devices in a mesh: gen: 8 (over z_lo, core), user: 16 (over x, y), cand: 2 (over z_hi).
Axes of the slice: x: 4, y: 4, z: 8 (z_hi: 2, z_lo: 4; z = z_hi * 4 + z_lo), core: 2. Of those that a mesh axis runs over, the one named last changes fastest.
Arguments:
- states: bfloat16 [16384, 4096], P(('user', 'cand')), may hold values from -6 to 6
- norm_gain: float32 [4096], replicated, may hold values from 0.1 to 1.9
- gate_weight: bfloat16 [4096, 7168], P('user', 'gen'), may hold values from -0.09375 to 0.09375
- up_weight: bfloat16 [4096, 7168], P('user', 'gen'), may hold values from -0.09375 to 0.09375
- down_weight: bfloat16 [7168, 4096], P('gen', 'user'), may hold values from -0.0625 to 0.0625
- proj_weight: bfloat16 [4096, 1024], P('gen'), may hold values from -0.09375 to 0.09375
- private_rows: bfloat16 [32768, 1024], P(('gen', 'user')), may hold values from -6 to 6
- enc_weight: bfloat16 [1024, 1024], replicated, may hold values from -0.1875 to 0.1875
- user_ids: int32 [32768], P(('gen', 'user')), may hold values from 0 to 31
Outputs:
- votes: float32 [16, 2, 128], P(None, 'cand')
Inputs may be any that keep to these rules, and one draw needn't show every extreme that they name: `user_ids`: a user is a pair of a block of 256 rows and a slot; no user has rows in two blocks.
All inputs are finite; a program needn't handle non-finite values.
Results may differ from a plain program's by a relative error of at most 0.0025.
Values may be sent and summed in bfloat16 or wider, within the bound.
No kernel may reach another device: no remote copies, remote signals or barrier semaphores. Data moves between devices by JAX's collectives and lax.ppermute only.
A program may use at most 128 MiB of HBM per device.

v0:
```python
import jax
import jax.numpy as jnp
from jax import lax
from jax.sharding import PartitionSpec as P

STEPS = 4
CAP = 8
USERS_DEV = 32


def unit_rows(matrix):
    return (matrix * lax.rsqrt(jnp.sum(matrix * matrix, axis=1, keepdims=True) + 1e-06)).astype(
        jnp.bfloat16
    )


def project_in(inputs, gate_part, up_part):

    def add_rows(piece):
        return jnp.dot(inputs, piece, preferred_element_type=jnp.float32)

    gate = add_rows(lax.all_gather(gate_part, "user", axis=0, tiled=True))
    up_proj = add_rows(lax.all_gather(up_part, "user", axis=0, tiled=True))
    return (gate, up_proj)


def shards(
    states,
    norm_gain,
    gate_weight,
    up_weight,
    down_weight,
    proj_weight,
    private_rows,
    enc_weight,
    user_ids,
):
    tok_rows, width_model = states.shape
    groups = tok_rows // STEPS
    values = states.astype(jnp.float32)
    normed = (
        values * lax.rsqrt(jnp.mean(values * values, axis=1, keepdims=True) + 1e-05) * norm_gain
    ).astype(jnp.bfloat16)
    gate_part, up_part, down_part = (gate_weight, up_weight, down_weight)
    gate, up_proj = project_in(normed, gate_part, up_part)
    hidden = (jax.nn.silu(gate) * up_proj).astype(jnp.bfloat16)
    mixed = jnp.dot(
        hidden,
        lax.all_gather(down_part, "user", axis=1, tiled=True),
        preferred_element_type=jnp.float32,
    )
    pooled_mlp = jnp.sum(mixed.reshape(-1, STEPS, width_model), axis=1)
    pooled_mlp = lax.psum_scatter(pooled_mlp, "gen", scatter_dimension=1, tiled=True)
    slab_width = pooled_mlp.shape[1]
    own_cols = lax.dynamic_slice_in_dim(values, lax.axis_index("gen") * slab_width, slab_width, 1)
    pooled_in = jnp.sum(own_cols.reshape(groups, STEPS, slab_width), axis=1)
    pooled = ((pooled_in + pooled_mlp) / STEPS).astype(jnp.bfloat16)
    partial_emb = jnp.dot(pooled, proj_weight, preferred_element_type=jnp.float32)
    embedding = lax.psum(partial_emb, "gen")
    candidate = unit_rows(embedding)
    every_cand = lax.all_gather(candidate, "user", axis=0, tiled=True)
    encoded = unit_rows(jnp.dot(private_rows, enc_weight, preferred_element_type=jnp.float32))
    scores = lax.dot_general(
        encoded, every_cand, (((1,), (1,)), ((), ())), preferred_element_type=jnp.float32
    )
    kernel = jnp.exp(scores * 60.0)
    totals = lax.psum(jnp.sum(kernel, axis=1), "cand")
    member = (user_ids[:, None] == jnp.arange(USERS_DEV, dtype=jnp.int32)[None, :]).astype(
        jnp.float32
    )
    counts = jnp.sum(member, axis=0)
    limit = jnp.minimum(1.0, CAP / jnp.maximum(counts, 1.0))
    row_cap = jnp.dot(member, limit, precision=lax.Precision.HIGHEST)
    row_total = private_rows.shape[0] * lax.axis_size("gen") * lax.axis_size("user")
    cand_total = every_cand.shape[0] * lax.axis_size("cand")
    weight_rows = row_cap / totals * (cand_total / row_total)
    partial_votes = jnp.dot(weight_rows, kernel, precision=lax.Precision.HIGHEST)
    votes = lax.psum(partial_votes, ("gen", "user"))
    return votes.reshape(lax.axis_size("user"), 1, groups)


def solution(mesh):
    return jax.shard_map(
        shards,
        mesh=mesh,
        in_specs=(
            P(("user", "cand"), None),
            P(),
            P("user", "gen"),
            P("user", "gen"),
            P("gen", "user"),
            P("gen", None),
            P(("gen", "user"), None),
            P(),
            P(("gen", "user")),
        ),
        out_specs=P(None, "cand", None),
        check_vma=False,
    )
```

profile of v0, /device:TPU:0, one launch (start us, length us, event | category | flops | bytes accessed | tf_op | source)
XLA Modules:
  0.0 810.1 jit_solution(10870717847516051505)
XLA Ops:
  6.5 0.7 all-gather.5.cloned.1.call-update
  7.3 0.0 all-gather.7.cloned.1.call-start
  7.3 0.7 all-gather.7.cloned.1.call-update
  8.1 0.7 all-gather.9.cloned.1.call-update
  8.7 0.0 reduce-scatter.2.cloned.1.call-start
  8.8 3.1 multiply_reduce_fusion
  11.9 70.3 %all-gather.5.cloned.1.call-done = bf16[4096,896]{1,0:T(8,128)(2,1)} async-done(((bf16[256,896]{1,0:T(8,128)(2,1)}), bf16[4096,896]{1,0:T(8,128)(2,1)}) %all-gather.5.cloned.1.call-update) | async-done | bytes 7340048 | tf_op jit(solution)/shard_map/all_gather | solution.py:22
  82.2 10.1 %fusion.1 = f32[512,896]{1,0:T(8,128)} fusion(bf16[4096,896]{1,0:T(8,128)(2,1)} %all-gather.5.cloned.1.call-done, f32[4096]{0:T(1024)S(1)} %copy-done.1, f32[512]{0:T(512)S(1)} %add_rsqrt_fusion, bf16[512,4096]{1,0:T(8,128)(2,1)} %param.9), kind=kOutput, calls=%fused_computation.5 | convolution fusion | flops 3766484992 | bytes 13387776 | tf_op jit(solution)/shard_map/dot_general | solution.py:20
  92.3 63.2 %all-gather.7.cloned.1.call-done = bf16[4096,896]{1,0:T(8,128)(2,1)} async-done(((bf16[256,896]{1,0:T(8,128)(2,1)}), bf16[4096,896]{1,0:T(8,128)(2,1)}) %all-gather.7.cloned.1.call-update) | async-done | bytes 7340048 | tf_op jit(solution)/shard_map/all_gather | solution.py:23
  155.6 79.3 %all-gather.9.cloned.1.call-done = bf16[896,4096]{1,0:T(8,128)(2,1)} async-done(((bf16[896,256]{1,0:T(8,128)(2,1)}), bf16[896,4096]{1,0:T(8,128)(2,1)}) %all-gather.9.cloned.1.call-update) | async-done | bytes 7340048 | tf_op jit(solution)/shard_map/all_gather | solution.py:49
  234.8 17.4 %fusion.2 = f32[512,4096]{1,0:T(8,128)} fusion(bf16[896,4096]{1,0:T(8,128)(2,1)} %all-gather.9.cloned.1.call-done, f32[512,896]{1,0:T(8,128)} %fusion.1, bf16[4096,896]{1,0:T(8,128)(2,1)} %all-gather.7.cloned.1.call-done, f32[4096]{0:T(1024)S(1)} %copy-done.1, f32[512]{0:T(512)S(1)} %add_rsqrt_fusion, bf16[512,4096]{1,0:T(8,128)(2,1)} %param.9), kind=kOutput, calls=%fused_computation.9 | convolution fusion | flops 7527333888 | bytes 29116416 | tf_op jit(solution)/shard_map/dot_general | solution.py:47
  252.2 9.8 %reshape.32 = f32[128,4,4096]{2,1,0:T(4,128)} reshape(f32[512,4096]{1,0:T(8,128)} %fusion.2) | data formatting | bytes 16777216 | tf_op jit(solution)/shard_map/reshape | solution.py:52
  262.0 10.0 %reduce_sum.67 = f32[128,4096]{1,0:T(8,128)} reduce(f32[128,4,4096]{2,1,0:T(4,128)} %reshape.32, f32[]{:T(128)} %constant.15.clone.1), dimensions={1}, to_apply=%region_4.5 | reduce | flops 1572864 | bytes 10485764 | tf_op jit(solution)/shard_map/reduce_sum | solution.py:52
  272.1 0.0 all-reduce.2.cloned.1.call-start
  272.1 6.5 convert_element_type.23
  278.6 1.3 constant_dynamic-slice_fusion
  279.9 1.3 reshape.31
  281.2 1.8 reduce_sum.65
  283.1 29.9 %reduce-scatter.2.cloned.1.call-done = f32[128,512]{1,0:T(8,128)} async-done(((f32[128,4096]{1,0:T(8,128)}), f32[128,512]{1,0:T(8,128)}) %reduce-scatter.2.cloned.1.call-update) | async-done | bytes 262160 | tf_op jit(solution)/shard_map/reduce_scatter | solution.py:53
  313.0 2.4 fusion.4
  315.4 0.3 all-gather.11.cloned.1.call-start
  315.7 70.7 %all-reduce.2.cloned.1.call-done = f32[128,1024]{1,0:T(8,128)} async-done(((f32[128,1024]{1,0:T(8,128)}), f32[128,1024]{1,0:T(8,128)}) %all-reduce.2.cloned.1.call-update) | async-done | bytes 524304 | tf_op jit(solution)/shard_map/psum | solution.py:59
  386.3 1.2 multiply_reduce_fusion.2
  387.5 1.8 multiply_convert_fusion.8
  389.4 0.1 convert_reduce_fusion
  389.5 1.8 multiply_reduce_fusion.1
  391.3 0.1 fusion.6
  391.5 53.5 %all-gather.11.cloned.1.call-done = bf16[2048,1024]{1,0:T(8,128)(2,1)} async-done(((bf16[128,1024]{1,0:T(8,128)(2,1)}), bf16[2048,1024]{1,0:T(8,128)(2,1)}) %all-gather.11.cloned.1.call-update) | async-done | bytes 4194320 | tf_op jit(solution)/shard_map/all_gather | solution.py:61
  445.0 4.9 fusion.16
  449.8 8.8 %psum.22 = f32[256]{0:T(256)S(1)} all-reduce(f32[256]{0:T(256)S(1)} %get-tuple-element.7), channel_id=1, replica_groups=mesh['gen'=8,'user'=16,'cand'=2] {'cand'}, use_global_device_ids=true, to_apply=%region_9.10 | all-reduce | flops 256 | bytes 2048 | tf_op jit(solution)/shard_map/psum | solution.py:67
  458.6 2.7 convolution_bitcast_fusion
  461.3 341.9 %psum.23 = f32[16,1,128]{2,1,0:T(1,128)} all-reduce(f32[16,1,128]{2,1,0:T(1,128)S(1)} %convolution_bitcast_fusion), channel_id=1, replica_groups=mesh['gen'=8,'user'=16,'cand'=2] {'gen','user'}, use_global_device_ids=true, to_apply=%region_10.11 | all-reduce | flops 2048 | bytes 16384 | tf_op jit(solution)/shard_map/psum | solution.py:78
  (15 shorter events, 0.1 us)
Async XLA Ops:
  6.5 383.0 %copy-start = (bf16[1024,1024]{1,0:T(8,128)(2,1)S(1)}, bf16[1024,1024]{1,0:T(8,128)(2,1)}, u32[]{:S(2)}) copy-start(bf16[1024,1024]{1,0:T(8,128)(2,1)} %param.16) | copy-start | bytes 6291460
  6.5 75.7 %copy-start.1 = (f32[4096]{0:T(1024)S(1)}, f32[4096]{0:T(1024)}, u32[]{:S(2)}) copy-start(f32[4096]{0:T(1024)} %param.10) | copy-start | bytes 49156
  6.5 75.7 %all-gather.5.cloned.1.call-start = ((), (), s32[]{:S(2)}) async-start(), calls=%async_computation.1 | async-start | bytes 7798784 | tf_op jit(solution)/shard_map/all_gather | solution.py:22
  7.3 148.3 %all-gather.7.cloned.1.call-start = ((), (), s32[]{:S(2)}) async-start(), calls=%async_computation.2 | async-start | bytes 7798784 | tf_op jit(solution)/shard_map/all_gather | solution.py:23
  8.0 226.8 %all-gather.9.cloned.1.call-start = ((), (), s32[]{:S(2)}) async-start(), calls=%async_computation.3 | async-start | bytes 7798784 | tf_op jit(solution)/shard_map/all_gather | solution.py:49
  8.7 304.2 %reduce-scatter.2.cloned.1.call-start = ((), (), s32[]{:S(2)}) async-start(), calls=%async_computation.4 | async-start | bytes 2359296 | tf_op jit(solution)/shard_map/reduce_scatter | solution.py:53
  272.1 114.3 %all-reduce.2.cloned.1.call-start = ((), (), s32[]{:S(2)}) async-start(), calls=%async_computation.5 | async-start | bytes 1048576 | tf_op jit(solution)/shard_map/psum | solution.py:59
  279.9 109.5 %copy-start.2 = (s32[256]{0:T(256)S(1)}, s32[256]{0:T(256)}, u32[]{:S(2)}) copy-start(s32[256]{0:T(256)} %param.17) | copy-start | bytes 3076
  315.4 129.5 %all-gather.11.cloned.1.call-start = ((), (), s32[]{:S(2)}) async-start(), calls=%async_computation.6 | async-start | bytes 4456448 | tf_op jit(solution)/shard_map/all_gather | solution.py:61
Sparse Core Ops, SparseCore 0:
  9.8 72.3 all-gather.4
  84.7 70.8 all-gather.6
  158.0 76.7 all-gather.8
  272.2 40.7 reduce-scatter.1
  315.5 70.7 all-reduce.1
  389.5 55.4 all-gather.10
where the time goes:
time: 811 us; the launch traced here: 810 us
  waiting for transfers between devices  369 us (45%)
  blocking collectives  351 us (43%)
  matrix products  39.5 us (5%)
  other arithmetic  24.6 us (3%)
  between operations  13.5 us (2%)
  local copies, waits for them, and re-layouts  12.4 us (2%)
    psum x1, blocking collectives, shards(): votes = lax.psum(partial_votes, ('gen', 'user'))  342 us
    all_gather x1, waiting for transfers between devices, shards(): lax.all_gather(down_part, 'user', axis=1, tiled=True)  79.3 us
    psum x1, waiting for transfers between devices, shards(): embedding = lax.psum(partial_emb, 'gen')  70.7 us
    all_gather x1, waiting for transfers between devices, project_in(): gate = add_rows(lax.all_gather(gate_part, 'user', axis=0, tiled=True))  70.3 us
    all_gather x1, waiting for transfers between devices, project_in(): up_proj = add_rows(lax.all_gather(up_part, 'user', axis=0, tiled=True))  63.2 us
    all_gather x1, waiting for transfers between devices, shards(): every_cand = lax.all_gather(candidate, 'user', axis=0, tiled=True)  53.5 us
    reduce_scatter x1, waiting for transfers between devices, shards(): lax.psum_scatter(pooled_mlp, 'gen', scatter_dimension=1, tiled=True)  29.9 us
    dot_general x1, matrix products, shards(): jnp.dot(hidden, lax.all_gather(down_part, 'user', axis=1, tiled=True), pr...  17.4 us
  transfers between devices with their start and end apart: 6, of which 6 were waited for; matrix products, arithmetic and copies ran while one was open for 3% of the time, Pallas kernels for 0%

commit v1 on v0

--- a/solution.py
+++ b/solution.py
@@ -75,7 +75,7 @@
     cand_total = every_cand.shape[0] * lax.axis_size("cand")
     weight_rows = row_cap / totals * (cand_total / row_total)
     partial_votes = jnp.dot(weight_rows, kernel, precision=lax.Precision.HIGHEST)
-    votes = lax.psum(partial_votes, ("gen", "user"))
+    votes = jnp.sum(lax.all_gather(partial_votes, ("gen", "user")), axis=0)
     return votes.reshape(lax.axis_size("user"), 1, groups)
 
 

time: 811 us -> 779 us (0.961)
  blocking collectives: 351 us -> 8.82 us
  waiting for transfers between devices: 369 us -> 673 us
    psum x1 -> x0, blocking collectives: 342 us -> none  [shards(): votes = lax.psum(partial_votes, ('gen', 'user'))]
    all_gather x0 -> x1, waiting for transfers between devices: none -> 304 us  [shards(): votes = jnp.sum(lax.all_gather(partial_votes, ('gen', 'user')), axis=0)]
  transfers between devices with their start and end apart: 6 -> 7, of which waited for: 6 -> 7; matrix products, arithmetic and copies ran while one was open for 3% -> 3% of each run, Pallas kernels for 0% -> 0%
where the time goes in v1:
time: 779 us; the launch traced here: 775 us
  waiting for transfers between devices  673 us (86%)
  matrix products  40.1 us (5%)
  other arithmetic  25.3 us (3%)
  local copies, waits for them, and re-layouts  13.8 us (2%)
  between operations  13.5 us (2%)
  blocking collectives  8.82 us (1%)
    all_gather x1, waiting for transfers between devices, shards(): votes = jnp.sum(lax.all_gather(partial_votes, ('gen', 'user')), axis=0)  304 us
    all_gather x1, waiting for transfers between devices, shards(): lax.all_gather(down_part, 'user', axis=1, tiled=True)  79.3 us
    psum x1, waiting for transfers between devices, shards(): embedding = lax.psum(partial_emb, 'gen')  70.9 us
    all_gather x1, waiting for transfers between devices, project_in(): gate = add_rows(lax.all_gather(gate_part, 'user', axis=0, tiled=True))  70.3 us
    all_gather x1, waiting for transfers between devices, project_in(): up_proj = add_rows(lax.all_gather(up_part, 'user', axis=0, tiled=True))  63.2 us
    all_gather x1, waiting for transfers between devices, shards(): every_cand = lax.all_gather(candidate, 'user', axis=0, tiled=True)  53.2 us
    reduce_scatter x1, waiting for transfers between devices, shards(): lax.psum_scatter(pooled_mlp, 'gen', scatter_dimension=1, tiled=True)  29.9 us
    dot_general x1, matrix products, shards(): jnp.dot(hidden, lax.all_gather(down_part, 'user', axis=1, tiled=True), pr...  17.4 us
  transfers between devices with their start and end apart: 7, of which 7 were waited for; matrix products, arithmetic and copies ran while one was open for 3% of the time, Pallas kernels for 0%

profile of v1, /device:TPU:0, one launch (start us, length us, event | category | flops | bytes accessed | tf_op | source)
XLA Modules:
  0.0 774.5 jit_solution(4845903373011978420)
XLA Ops:
  6.5 0.7 all-gather.7.cloned.1.call-update
  7.3 0.7 all-gather.9.cloned.1.call-update
  8.1 0.7 all-gather.11.cloned.1.call-update
  8.8 3.1 multiply_reduce_fusion
  11.9 70.3 %all-gather.7.cloned.1.call-done = bf16[4096,896]{1,0:T(8,128)(2,1)} async-done(((bf16[256,896]{1,0:T(8,128)(2,1)}), bf16[4096,896]{1,0:T(8,128)(2,1)}) %all-gather.7.cloned.1.call-update) | async-done | bytes 7340048 | tf_op jit(solution)/shard_map/all_gather | solution.py:22
  82.2 10.1 %fusion.1 = f32[512,896]{1,0:T(8,128)} fusion(bf16[4096,896]{1,0:T(8,128)(2,1)} %all-gather.7.cloned.1.call-done, f32[4096]{0:T(1024)S(1)} %copy-done.1, f32[512]{0:T(512)S(1)} %add_rsqrt_fusion, bf16[512,4096]{1,0:T(8,128)(2,1)} %param.9), kind=kOutput, calls=%fused_computation.5 | convolution fusion | flops 3766484992 | bytes 13387776 | tf_op jit(solution)/shard_map/dot_general | solution.py:20
  92.3 63.2 %all-gather.9.cloned.1.call-done = bf16[4096,896]{1,0:T(8,128)(2,1)} async-done(((bf16[256,896]{1,0:T(8,128)(2,1)}), bf16[4096,896]{1,0:T(8,128)(2,1)}) %all-gather.9.cloned.1.call-update) | async-done | bytes 7340048 | tf_op jit(solution)/shard_map/all_gather | solution.py:23
  155.6 79.3 %all-gather.11.cloned.1.call-done = bf16[896,4096]{1,0:T(8,128)(2,1)} async-done(((bf16[896,256]{1,0:T(8,128)(2,1)}), bf16[896,4096]{1,0:T(8,128)(2,1)}) %all-gather.11.cloned.1.call-update) | async-done | bytes 7340048 | tf_op jit(solution)/shard_map/all_gather | solution.py:49
  234.8 17.4 %fusion.2 = f32[512,4096]{1,0:T(8,128)} fusion(bf16[896,4096]{1,0:T(8,128)(2,1)} %all-gather.11.cloned.1.call-done, f32[512,896]{1,0:T(8,128)} %fusion.1, bf16[4096,896]{1,0:T(8,128)(2,1)} %all-gather.9.cloned.1.call-done, f32[4096]{0:T(1024)S(1)} %copy-done.1, f32[512]{0:T(512)S(1)} %add_rsqrt_fusion, bf16[512,4096]{1,0:T(8,128)(2,1)} %param.9), kind=kOutput, calls=%fused_computation.8 | convolution fusion | flops 7527333888 | bytes 29116416 | tf_op jit(solution)/shard_map/dot_general | solution.py:47
  252.2 9.8 %reshape.32 = f32[128,4,4096]{2,1,0:T(4,128)} reshape(f32[512,4096]{1,0:T(8,128)} %fusion.2) | data formatting | bytes 16777216 | tf_op jit(solution)/shard_map/reshape | solution.py:52
  262.0 10.0 %reduce_sum.76 = f32[128,4096]{1,0:T(8,128)} reduce(f32[128,4,4096]{2,1,0:T(4,128)} %reshape.32, f32[]{:T(128)} %constant.15.clone.1), dimensions={1}, to_apply=%region_4.5 | reduce | flops 1572864 | bytes 10485764 | tf_op jit(solution)/shard_map/reduce_sum | solution.py:52
  272.1 6.5 convert_element_type.23
  278.6 1.3 constant_dynamic-slice_fusion
  279.9 1.3 reshape.31
  281.2 1.8 reduce_sum.74
  283.1 29.9 %reduce-scatter.2.cloned.1.call-done = f32[128,512]{1,0:T(8,128)} async-done(((f32[128,4096]{1,0:T(8,128)}), f32[128,512]{1,0:T(8,128)}) %reduce-scatter.2.cloned.1.call-update) | async-done | bytes 262160 | tf_op jit(solution)/shard_map/reduce_scatter | solution.py:53
  313.0 2.4 fusion.4
  315.4 0.0 all-gather.13.cloned.1.call-start
  315.5 70.9 %all-reduce.2.cloned.1.call-done = f32[128,1024]{1,0:T(8,128)} async-done(((f32[128,1024]{1,0:T(8,128)}), f32[128,1024]{1,0:T(8,128)}) %all-reduce.2.cloned.1.call-update) | async-done | bytes 524304 | tf_op jit(solution)/shard_map/psum | solution.py:59
  386.3 1.2 multiply_reduce_fusion.2
  387.5 1.8 multiply_convert_fusion.8
  389.4 0.3 all-gather.15.cloned.1.call-start
  389.7 0.1 convert_reduce_fusion
  389.8 1.8 multiply_reduce_fusion.1
  391.6 0.1 fusion.6
  391.8 53.2 %all-gather.13.cloned.1.call-done = bf16[2048,1024]{1,0:T(8,128)(2,1)} async-done(((bf16[128,1024]{1,0:T(8,128)(2,1)}), bf16[2048,1024]{1,0:T(8,128)(2,1)}) %all-gather.13.cloned.1.call-update) | async-done | bytes 4194320 | tf_op jit(solution)/shard_map/all_gather | solution.py:61
  445.0 4.9 fusion.16
  449.8 8.8 %psum.15 = f32[256]{0:T(256)S(1)} all-reduce(f32[256]{0:T(256)S(1)} %get-tuple-element.7), channel_id=1, replica_groups=mesh['gen'=8,'user'=16,'cand'=2] {'cand'}, use_global_device_ids=true, to_apply=%region_9.10 | all-reduce | flops 256 | bytes 2048 | tf_op jit(solution)/shard_map/psum | solution.py:67
  458.6 3.3 fusion.17
  462.0 303.7 %all-gather.15.cloned.1.call-done = f32[262144]{0:T(1024)} async-done(((f32[2048]{0:T(1024)}), f32[262144]{0:T(1024)}) %all-gather.15.cloned.1.call-update) | async-done | bytes 1048592 | tf_op jit(solution)/shard_map/all_gather | solution.py:78
  765.6 1.4 reshape.34
  767.0 0.7 reduce_sum.79
  (19 shorter events, 0.3 us)
Async XLA Ops:
  6.5 383.2 %copy-start = (bf16[1024,1024]{1,0:T(8,128)(2,1)S(1)}, bf16[1024,1024]{1,0:T(8,128)(2,1)}, u32[]{:S(2)}) copy-start(bf16[1024,1024]{1,0:T(8,128)(2,1)} %param.16) | copy-start | bytes 6291460
  6.5 75.7 %copy-start.1 = (f32[4096]{0:T(1024)S(1)}, f32[4096]{0:T(1024)}, u32[]{:S(2)}) copy-start(f32[4096]{0:T(1024)} %param.10) | copy-start | bytes 49156
  6.5 75.7 %all-gather.7.cloned.1.call-start = ((), (), s32[]{:S(2)}) async-start(), calls=%async_computation.1 | async-start | bytes 7798784 | tf_op jit(solution)/shard_map/all_gather | solution.py:22
  7.3 148.3 %all-gather.9.cloned.1.call-start = ((), (), s32[]{:S(2)}) async-start(), calls=%async_computation.2 | async-start | bytes 7798784 | tf_op jit(solution)/shard_map/all_gather | solution.py:23
  8.0 226.8 %all-gather.11.cloned.1.call-start = ((), (), s32[]{:S(2)}) async-start(), calls=%async_computation.3 | async-start | bytes 7798784 | tf_op jit(solution)/shard_map/all_gather | solution.py:49
  8.7 304.2 %reduce-scatter.2.cloned.1.call-start = ((), (), s32[]{:S(2)}) async-start(), calls=%async_computation.4 | async-start | bytes 2359296 | tf_op jit(solution)/shard_map/reduce_scatter | solution.py:53
  272.1 114.3 %all-reduce.2.cloned.1.call-start = ((), (), s32[]{:S(2)}) async-start(), calls=%async_computation.5 | async-start | bytes 1048576 | tf_op jit(solution)/shard_map/psum | solution.py:59
  279.9 109.7 %copy-start.2 = (s32[256]{0:T(256)S(1)}, s32[256]{0:T(256)}, u32[]{:S(2)}) copy-start(s32[256]{0:T(256)} %param.17) | copy-start | bytes 3076
  315.4 129.5 %all-gather.13.cloned.1.call-start = ((), (), s32[]{:S(2)}) async-start(), calls=%async_computation.6 | async-start | bytes 4456448 | tf_op jit(solution)/shard_map/all_gather | solution.py:61
  389.4 376.3 %all-gather.15.cloned.1.call-start = ((), (), s32[]{:S(2)}) async-start(), calls=%async_computation.7 | async-start | bytes 1056768 | tf_op jit(solution)/shard_map/all_gather | solution.py:78
Sparse Core Ops, SparseCore 0:
  9.8 72.3 all-gather.6
  84.7 70.8 all-gather.8
  158.0 76.7 all-gather.10
  272.2 40.7 reduce-scatter.1
  315.5 70.7 all-reduce.1
  389.5 55.4 all-gather.12
  462.1 303.5 all-gather.14
